TPU v7x, 128 devices: a whole 4x4x4 slice. The times are simulated.
128 devices in a mesh: row: 8 (over z, core), col: 16 (over y, x).
Axes of the slice: x: 4, y: 4, z: 4, core: 2. Of those that a mesh axis runs over, the one named last changes fastest.
Arguments:
- snapshots: bfloat16 [4096, 32768], P('row', 'col'), may hold values from -14 to 14
- neighbours: int32 [4096, 128], P('row'), may hold values from 0 to 4095, all different within a row
- start_basis: float32 [32, 4096], replicated, may hold values from -6 to 6
Outputs:
- basis: float32 [32, 4096], P(None, 'row')
- rayleigh: float32 [32, 32], replicated
Inputs may be any that keep to these rules, and one draw needn't show every extreme that they name: `neighbours`: each row names 128 different snapshots.
All inputs are finite; a program needn't handle non-finite values.
Results may differ from a plain program's by a relative error of at most 0.00145.
Values may be sent and summed in bfloat16 or wider, within the bound.
No kernel may reach another device: no remote copies, remote signals or barrier semaphores. Data moves between devices by JAX's collectives and lax.ppermute only.
A program may use at most 128 MiB of HBM per device.

v0:
```python
import math
import jax
import jax.numpy as jnp
from jax import lax
from jax.sharding import PartitionSpec as P

FEATURES = 32768
LAGS = 64
ITERS = 2


def global_sum(value):
    return lax.psum(value, ("row", "col"))


def collect(columns):
    return lax.all_gather(columns, ("row", "col"), axis=1, tiled=True)


def shards(snapshots, neighbours, start_basis):
    row_count = lax.axis_size("row")
    col_count = lax.axis_size("col")
    row_at = lax.axis_index("row")
    col_at = lax.axis_index("col")
    lag_count = LAGS
    whole = lax.all_gather(snapshots, "row", axis=0, tiled=True)
    snap_count = whole.shape[0]
    feat_width = whole.shape[1]
    col_block = snap_count // col_count
    row_block = snapshots.shape[0]
    squares = jnp.sum(jnp.square(whole.astype(jnp.float32)), axis=1)
    padded_rows = jnp.concatenate([jnp.zeros((lag_count, feat_width), whole.dtype), whole], 0)
    padded_norms = jnp.concatenate([jnp.zeros((lag_count,), jnp.float32), squares], 0)
    row_start = row_at * row_block
    ext_rows = lax.dynamic_slice_in_dim(padded_rows, row_start, row_block + lag_count, 0)
    ext_norms = lax.dynamic_slice_in_dim(padded_norms, row_start, row_block + lag_count, 0)
    row_times = row_start - lag_count + jnp.arange(row_block + lag_count, dtype=jnp.int32)
    span = col_block + lag_count
    blocks = whole.reshape(col_count, col_block, feat_width)
    earlier = jnp.concatenate(
        [jnp.zeros((1, lag_count, feat_width), whole.dtype), blocks[:-1, col_block - lag_count :]],
        0,
    )
    source_rows = jnp.concatenate([earlier, blocks], 1).reshape(col_count * span, feat_width)
    norm_blocks = squares.reshape(col_count, col_block)
    norm_earlier = jnp.concatenate(
        [jnp.zeros((1, lag_count), jnp.float32), norm_blocks[:-1, col_block - lag_count :]], 0
    )
    source_norms = jnp.concatenate([norm_earlier, norm_blocks], 1).reshape(col_count * span)
    virtual = jnp.arange(span * lax.axis_size("col"), dtype=jnp.int32)
    times = virtual // span * col_block + virtual % span - lag_count
    inner = lax.dot_general(
        source_rows, ext_rows, (((1,), (1,)), ((), ())), preferred_element_type=jnp.float32
    )
    term = source_norms[:, None] + ext_norms[None, :] - 2.0 * inner
    keep = (times >= 0)[:, None] & (row_times >= 0)[None, :]
    tile = lax.psum_scatter(
        jnp.where(keep, term, 0.0).astype(jnp.bfloat16), "col", scatter_dimension=0, tiled=True
    ).astype(jnp.float32)
    window = 1
    while window < lag_count:
        tile = tile[window:, window:] + tile[:-window, :-window]
        window = window * 2
    lagged = tile[1:, 1:]
    step_rows = math.gcd(row_block, 16)
    block_count = row_block // step_rows
    slot_count = neighbours.shape[1]
    offset = neighbours - col_at * col_block
    inside = (offset >= 0) & (offset < col_block)
    tile_positions = jnp.arange(col_block, dtype=jnp.int32)

    def pick_block(pair):
        offs, lag_rows = pair
        match = offs[:, :, None] == tile_positions[None, None, :]
        return jnp.sum(jnp.where(match, lag_rows[:, None, :], 0.0), axis=2)

    chosen = lax.map(
        pick_block,
        (
            offset.reshape(block_count, step_rows, slot_count),
            lagged.T.reshape(block_count, step_rows, col_block),
        ),
    )
    chosen = chosen.reshape(row_block, slot_count)
    kernel_part = jnp.where(inside, 1.0 / (1.0 + chosen / (LAGS * FEATURES)), 0.0)
    slot_kernel = lax.psum(kernel_part, "col")
    mass = jnp.sum(slot_kernel, axis=1)
    markov = slot_kernel / mass[:, None]
    snap_positions = jnp.arange(snap_count, dtype=jnp.int32)

    def operator_block(pair):
        ids, weights = pair
        match = ids[:, :, None] == snap_positions[None, None, :]
        return jnp.sum(jnp.where(match, weights[:, :, None], 0.0), axis=1)

    transition = lax.map(
        operator_block,
        (
            neighbours.reshape(block_count, step_rows, slot_count),
            markov.reshape(block_count, step_rows, slot_count),
        ),
    )
    transition = transition.reshape(row_block, snap_count)
    piece_width = snap_count // (row_count * col_count)

    def apply_rows(basis_rows):
        return lax.dot_general(
            basis_rows,
            transition,
            (((1,), (1,)), ((), ())),
            precision=lax.Precision.HIGHEST,
            preferred_element_type=jnp.float32,
        )

    def own_piece(image):
        return lax.dynamic_slice_in_dim(image, col_at * piece_width, piece_width, 1)

    basis = start_basis
    for step in range(ITERS):
        piece = own_piece(apply_rows(basis))
        partial_gram = jnp.dot(
            piece, piece.T, precision=lax.Precision.HIGHEST, preferred_element_type=jnp.float32
        )
        gram_small = global_sum(partial_gram) / snap_count
        lower = jnp.linalg.cholesky(gram_small)
        basis = collect(jax.scipy.linalg.solve_triangular(lower, piece, lower=True))
    image_piece = own_piece(apply_rows(basis))
    basis_piece = lax.dynamic_slice_in_dim(
        basis, (row_at * col_count + col_at) * piece_width, piece_width, 1
    )
    partial_ray = jnp.dot(
        basis_piece,
        image_piece.T,
        precision=lax.Precision.HIGHEST,
        preferred_element_type=jnp.float32,
    )
    rayleigh = global_sum(partial_ray) / snap_count
    basis_rows = lax.dynamic_slice_in_dim(basis, row_start, row_block, 1)
    return (basis_rows, rayleigh)


def solution(mesh):
    placed = (P("row", "col"), P("row", None), P())
    return jax.shard_map(
        shards, mesh=mesh, in_specs=placed, out_specs=(P(None, "row"), P()), check_vma=False
    )
```

profile of v0, /device:TPU:1, one launch (start us, length us, event | category | flops | bytes accessed | tf_op | source)
XLA Modules:
  0.0 1007.9 jit_solution(16402256858035387622)
XLA Ops:
  8.0 90.6 %all-gather.2.cloned.1.call-done = bf16[4096,2048]{1,0:T(8,128)(2,1)} async-done(((bf16[512,2048]{1,0:T(8,128)(2,1)}), bf16[4096,2048]{1,0:T(8,128)(2,1)}) %all-gather.2.cloned.1.call-update) | async-done | bytes 16777232 | tf_op jit(solution)/shard_map/all_gather | solution.py:26
  98.6 7.2 multiply_reduce_fusion
  108.7 21.4 %fusion.5 = bf16[16,320,2048]{2,1,0:T(8,128)(2,1)} fusion(bf16[15,64,2048]{2,1,0:T(8,128)(2,1)S(1)} %slice.69, bf16[16,256,2048]{2,1,0:T(8,128)(2,1)} %bitcast.64), kind=kLoop, calls=%fused_computation.15 | loop fusion | flops 62914560 | bytes 41680896 | tf_op jit(solution)/shard_map/concatenate | solution.py:44
  130.2 23.8 %select_convert_fusion = bf16[5120,576]{1,0:T(8,128)(2,1)} fusion(bf16[5120,2048]{1,0:T(8,128)(2,1)} %bitcast.70, f32[576]{0:T(1024)S(1)} %pad_dynamic-slice_fusion.2, f32[5120]{0:T(1024)S(1)} %add.130, pred[576]{0:T(1024)(128)(4,1)S(1)} %add_compare_fusion, pred[5120]{0:T(1024)(128)(4,1)S(1)} %fusion.17, s32[]{:T(128)S(6)} %select_n.56, ...), kind=kOutput, calls=%fused_computation.17 | convolution fusion | flops 12097290240 | bytes 43675460 | tf_op jit(solution)/shard_map/dot_general | solution.py:52
  154.1 80.7 %reduce-scatter.2.cloned.1.call-done = bf16[320,576]{1,0:T(8,128)(2,1)} async-done(((bf16[5120,576]{1,0:T(8,128)(2,1)}), bf16[320,576]{1,0:T(8,128)(2,1)}) %reduce-scatter.2.cloned.1.call-update) | async-done | bytes 368656 | tf_op jit(solution)/shard_map/reduce_scatter | solution.py:57
  238.1 28.1 %while.22 = (s32[]{:T(128)}, f32[32,16,128]{2,1,0:T(8,128)S(1)}, s32[32,16,128]{2,1,0:T(8,128)S(1)}, f32[32,16,256]{2,1,0:T(8,128)S(1)}, s32[]{:T(128)}) while((s32[]{:T(128)}, f32[32,16,128]{2,1,0:T(8,128)S(1)}, s32[32,16,128]{2,1,0:T(8,128)S(1)}, f32[32,16,256]{2,1,0:T(8,128)S(1)}, s32[]{:T(128)}) %tuple.63), condition=%wide.region_4.5_spmd.clone, body=%wide.region_2.4_spmd.clone.sunk | while | flops 1570818 | bytes 98377 | solution.py:77
  267.0 83.3 %all-reduce.6.cloned.1.call-done = f32[512,128]{1,0:T(8,128)} async-done(((f32[512,128]{1,0:T(8,128)}), f32[512,128]{1,0:T(8,128)}) %all-reduce.6.cloned.1.call-update) | async-done | bytes 262160 | tf_op jit(solution)/shard_map/psum | solution.py:86
  352.5 280.2 %while.23 = (s32[]{:T(128)}, f32[32,16,4096]{2,1,0:T(8,128)}, s32[32,16,128]{2,1,0:T(8,128)S(1)}, f32[32,16,128]{2,1,0:T(8,128)S(1)}, s32[]{:T(128)}) while((s32[]{:T(128)}, f32[32,16,4096]{2,1,0:T(8,128)}, s32[32,16,128]{2,1,0:T(8,128)S(1)}, f32[32,16,128]{2,1,0:T(8,128)S(1)}, s32[]{:T(128)}) %tuple.64), condition=%wide.region_9.10_spmd.clone, body=%wide.region_7.9_spmd.clone.sunk | while | flops 25100288 | bytes 836165 | solution.py:96
  352.6 8.0 select_reduce_fusion.6
  361.3 8.0 select_reduce_fusion.6
  370.0 8.0 select_reduce_fusion.6
  378.8 8.0 select_reduce_fusion.6
  387.5 8.0 select_reduce_fusion.6
  396.3 8.0 select_reduce_fusion.6
  405.1 8.0 select_reduce_fusion.6
  413.8 8.0 select_reduce_fusion.6
  422.6 8.0 select_reduce_fusion.6
  431.4 8.0 select_reduce_fusion.6
  440.1 8.0 select_reduce_fusion.6
  448.9 8.0 select_reduce_fusion.6
  457.6 8.0 select_reduce_fusion.6
  466.4 8.0 select_reduce_fusion.6
  475.1 8.0 select_reduce_fusion.6
  483.9 8.0 select_reduce_fusion.6
  492.6 8.0 select_reduce_fusion.6
  501.4 8.0 select_reduce_fusion.6
  510.1 8.0 select_reduce_fusion.6
  518.9 8.0 select_reduce_fusion.6
  527.7 8.0 select_reduce_fusion.6
  536.4 8.0 select_reduce_fusion.6
  545.2 8.0 select_reduce_fusion.6
  553.9 8.0 select_reduce_fusion.6
  562.7 8.0 select_reduce_fusion.6
  571.4 8.0 select_reduce_fusion.6
  580.2 8.0 select_reduce_fusion.6
  589.0 8.0 select_reduce_fusion.6
  597.7 8.0 select_reduce_fusion.6
  606.5 8.0 select_reduce_fusion.6
  615.2 8.0 select_reduce_fusion.6
  623.9 8.0 select_reduce_fusion.6
  632.7 9.2 fusion.46
  642.1 65.8 %psum.29 = f32[32,32]{0,1:T(8,128)S(1)} all-reduce(f32[32,32]{0,1:T(8,128)S(1)} %fusion.36), channel_id=1, replica_groups=mesh['row'=8,'col'=16] {'row','col'}, use_global_device_ids=true, to_apply=%region_10.11 | all-reduce | flops 1024 | bytes 8192 | tf_op jit(solution)/shard_map/psum | solution.py:13
  714.8 63.7 %all_gather.10 = f32[32,4096]{0,1:T(8,128)S(1)} all-gather(f32[32,32]{0,1:T(8,128)S(1)} %fusion.23), channel_id=1, replica_groups=mesh['row'=8,'col'=16] {'row','col'}, dimensions={1}, use_global_device_ids=true | all-gather | bytes 528384 | tf_op jit(solution)/shard_map/all_gather | solution.py:17
  778.6 9.3 fusion.47
  788.1 65.0 %psum.30 = f32[32,32]{0,1:T(8,128)S(1)} all-reduce(f32[32,32]{0,1:T(8,128)S(1)} %fusion.33), channel_id=1, replica_groups=mesh['row'=8,'col'=16] {'row','col'}, use_global_device_ids=true, to_apply=%region_13.16 | all-reduce | flops 1024 | bytes 8192 | tf_op jit(solution)/shard_map/psum | solution.py:13
  860.2 65.1 %all_gather.11 = f32[32,4096]{0,1:T(8,128)S(1)} all-gather(f32[32,32]{0,1:T(8,128)S(1)} %fusion.20), channel_id=1, replica_groups=mesh['row'=8,'col'=16] {'row','col'}, dimensions={1}, use_global_device_ids=true | all-gather | bytes 528384 | tf_op jit(solution)/shard_map/all_gather | solution.py:17
  925.3 9.2 fusion.48
  934.8 65.0 %psum.31 = f32[32,32]{0,1:T(8,128)S(1)} all-reduce(f32[32,32]{0,1:T(8,128)S(1)} %fusion.29), channel_id=1, replica_groups=mesh['row'=8,'col'=16] {'row','col'}, use_global_device_ids=true, to_apply=%region_14.17 | all-reduce | flops 1024 | bytes 8192 | tf_op jit(solution)/shard_map/psum | solution.py:13
  (292 shorter events, 75.8 us)
Async XLA Ops:
  7.2 625.5 %copy-start = (f32[32,4096]{1,0:T(8,128)S(1)}, f32[32,4096]{1,0:T(8,128)}, u32[]{:S(2)}) copy-start(f32[32,4096]{1,0:T(8,128)} %param.12) | copy-start | bytes 1572868
  7.2 91.4 %all-gather.2.cloned.1.call-start = ((), (), s32[]{:S(2)}) async-start(), calls=%async_computation.1 | async-start | bytes 18874368 | tf_op jit(solution)/shard_map/all_gather | solution.py:26
  7.9 226.8 %reduce-scatter.2.cloned.1.call-start = ((), (), s32[]{:S(2)}) async-start(), calls=%async_computation.2 | async-start | bytes 6963200 | tf_op jit(solution)/shard_map/reduce_scatter | solution.py:57
  106.1 24.0 %slice-start = ((s8[16777216]{0:T(1024)(128)(4,1)}), s8[4194304]{0:T(1024)(128)(4,1)S(1)}, s32[]{:S(2)}) async-start(s8[16777216]{0:T(1024)(128)(4,1)} %bitcast.65), calls=%async_computation.4 | async-start | bytes 8388608
  108.7 21.5 %slice-start.1 = ((s8[16777216]{0:T(1024)(128)(4,1)}), s8[4194304]{0:T(1024)(128)(4,1)S(1)}, s32[]{:S(2)}) async-start(s8[16777216]{0:T(1024)(128)(4,1)} %bitcast.65), calls=%async_computation.5 | async-start | bytes 8388608
  108.7 21.4 %slice-start.2 = ((s8[16777216]{0:T(1024)(128)(4,1)}), s8[4194304]{0:T(1024)(128)(4,1)S(1)}, s32[]{:S(2)}) async-start(s8[16777216]{0:T(1024)(128)(4,1)} %bitcast.65), calls=%async_computation.6 | async-start | bytes 8388608
  108.7 21.4 %slice-start.3 = ((s8[16777216]{0:T(1024)(128)(4,1)}), s8[4194304]{0:T(1024)(128)(4,1)S(1)}, s32[]{:S(2)}) async-start(s8[16777216]{0:T(1024)(128)(4,1)} %bitcast.65), calls=%async_computation.7 | async-start | bytes 8388608
  130.1 23.9 %copy-start.1 = (s32[512,128]{1,0:T(8,128)S(1)}, s32[512,128]{1,0:T(8,128)}, u32[]{:S(2)}) copy-start(s32[512,128]{1,0:T(8,128)} %param.11) | copy-start | bytes 786436
  154.0 196.3 %all-reduce.6.cloned.1.call-start = ((), (), s32[]{:S(2)}) async-start(), calls=%async_computation.3 | async-start | bytes 524288 | tf_op jit(solution)/shard_map/psum | solution.py:86
Sparse Core Ops, SparseCore 0:
  9.7 88.8 all-gather.1
  154.1 80.6 reduce-scatter.1
  267.1 83.1 all-reduce.5
where the time goes:
time: 1020 us; the launch traced here: 1010 us
  other arithmetic  330 us (32%)
  blocking collectives  325 us (32%)
  waiting for transfers between devices  255 us (25%)
  matrix products  52.6 us (5%)
  local copies, waits for them, and re-layouts  29.2 us (3%)
  between operations  14.3 us (1%)
    reduce_sum x32, other arithmetic, operator_block(): return jnp.sum(jnp.where(match, weights[:, :, None], 0.0), axis=1)  256 us
    psum x3, blocking collectives, global_sum(): return lax.psum(value, ('row', 'col'))  196 us
    all_gather x2, blocking collectives, collect(): return lax.all_gather(columns, ('row', 'col'), axis=1, tiled=True)  129 us
    all_gather x1, waiting for transfers between devices, shards(): whole = lax.all_gather(snapshots, 'row', axis=0, tiled=True)  90.6 us
    psum x1, waiting for transfers between devices, shards(): slot_kernel = lax.psum(kernel_part, 'col')  83.3 us
    reduce_scatter x1, waiting for transfers between devices, shards(): lax.psum_scatter(jnp.where(keep, term, 0.0).astype(jnp.bfloat16), 'col',...  80.7 us
    dot_general x3, matrix products, apply_rows(): lax.dot_general(basis_rows, transition, (((1,), (1,)), ((), ())), precisi...  27.6 us
    reduce_sum x32, other arithmetic, pick_block(): return jnp.sum(jnp.where(match, lag_rows[:, None, :], 0.0), axis=2)  25.3 us
  transfers between devices with their start and end apart: 3, of which 3 were waited for; matrix products, arithmetic and copies ran while one was open for 0% of the time, Pallas kernels for 0%

commit v1 on v0

--- a/solution.py
+++ b/solution.py
@@ -7,6 +7,12 @@
 FEATURES = 32768
 LAGS = 64
 ITERS = 2
+
+
+def laid_out(blocks, dim):
+    shape = list(blocks.shape[1:])
+    shape[dim] *= blocks.shape[0]
+    return jnp.moveaxis(blocks, 0, dim).reshape(shape)
 
 
 def global_sum(value):
@@ -23,7 +29,19 @@
     row_at = lax.axis_index("row")
     col_at = lax.axis_index("col")
     lag_count = LAGS
-    whole = lax.all_gather(snapshots, "row", axis=0, tiled=True)
+    size = lax.axis_size("row")
+    pairs = [(i, (i + 1) % size) for i in range(size)]
+    back = [(b, a) for a, b in pairs]
+    lower_2, upper = ([], [])
+    for step_2 in range(size - 1):
+        if step_2 % 2 == 0:
+            lower_2.append(lax.ppermute(lower_2[-1] if lower_2 else snapshots, "row", pairs))
+        else:
+            upper.append(lax.ppermute(upper[-1] if upper else snapshots, "row", back))
+    blocks_2 = jnp.stack([*lower_2[::-1], snapshots, *upper])
+    shift = lax.axis_index("row") - len(lower_2)
+    blocks_2 = blocks_2[(jnp.arange(size) - shift) % size]
+    whole = laid_out(blocks_2, 0)
     snap_count = whole.shape[0]
     feat_width = whole.shape[1]
     col_block = snap_count // col_count

time: 1020 us -> 1080 us (1.059)
  local copies, waits for them, and re-layouts: 29.2 us -> 76.1 us
  starting transfers between devices: 0.12 us -> 14.6 us
    all_gather x1 -> x0, waiting for transfers between devices: 90.6 us -> none  [shards(): whole = lax.all_gather(snapshots, 'row', axis=0, tiled=True)]
    ppermute x0 -> x7, waiting for transfers between devices: none -> 88.6 us  [the longest x4 88.1 us: shards(): lax.ppermute(lower_2[-1] if lower_2 else snapshots, 'row', pairs)]
    unnamed x14 -> x30, local copies, waits for them, and re-layouts: 1.45 us -> 25.8 us
    gather x0 -> x3, local copies, waits for them, and re-layouts: none -> 22.5 us  [shards(): blocks_2 = blocks_2[(jnp.arange(size) - shift) % size]]
    ppermute x0 -> x7, starting transfers between devices: none -> 14.4 us  [the longest x4 10.5 us: shards(): lax.ppermute(lower_2[-1] if lower_2 else snapshots, 'row', pairs)]
  transfers between devices with their start and end apart: 3 -> 9, of which waited for: 3 -> 7; matrix products, arithmetic and copies ran while one was open for 0% -> 1% of each run, Pallas kernels for 0% -> 0%
where the time goes in v1:
time: 1080 us; the launch traced here: 1070 us
  other arithmetic  330 us (31%)
  blocking collectives  325 us (30%)
  waiting for transfers between devices  257 us (24%)
  local copies, waits for them, and re-layouts  76.1 us (7%)
  matrix products  52.6 us (5%)
  between operations  14.9 us (1%)
  starting transfers between devices  14.6 us (1%)
    reduce_sum x32, other arithmetic, operator_block(): return jnp.sum(jnp.where(match, weights[:, :, None], 0.0), axis=1)  256 us
    psum x3, blocking collectives, global_sum(): return lax.psum(value, ('row', 'col'))  196 us
    all_gather x2, blocking collectives, collect(): return lax.all_gather(columns, ('row', 'col'), axis=1, tiled=True)  129 us
    ppermute x4, waiting for transfers between devices, shards(): lax.ppermute(lower_2[-1] if lower_2 else snapshots, 'row', pairs)  88.1 us
    reduce_scatter x1, waiting for transfers between devices, shards(): lax.psum_scatter(jnp.where(keep, term, 0.0).astype(jnp.bfloat16), 'col',...  85 us
    psum x1, waiting for transfers between devices, shards(): slot_kernel = lax.psum(kernel_part, 'col')  83.3 us
    dot_general x3, matrix products, apply_rows(): lax.dot_general(basis_rows, transition, (((1,), (1,)), ((), ())), precisi...  27.7 us
    unnamed x30, local copies, waits for them, and re-layouts  25.8 us
  transfers between devices with their start and end apart: 9, of which 7 were waited for; matrix products, arithmetic and copies ran while one was open for 1% of the time, Pallas kernels for 0%

profile of v1, /device:TPU:1, one launch (start us, length us, event | category | flops | bytes accessed | tf_op | source)
XLA Modules:
  0.0 1071.2 jit_solution(553689574083091835)
XLA Ops:
  10.3 23.3 %collective-permute-done = bf16[512,2048]{1,0:T(8,128)(2,1)S(1)} collective-permute-done((bf16[512,2048]{1,0:T(8,128)(2,1)}, bf16[512,2048]{1,0:T(8,128)(2,1)S(1)}, u32[]{:S(2)}, u32[]{:S(2)}) %collective-permute-start) | collective-permute-done | bytes 2097184 | tf_op jit(solution)/shard_map/ppermute | solution.py:38
  36.2 22.8 %collective-permute-done.1 = bf16[512,2048]{1,0:T(8,128)(2,1)S(1)} collective-permute-done((bf16[512,2048]{1,0:T(8,128)(2,1)S(1)}, bf16[512,2048]{1,0:T(8,128)(2,1)S(1)}, u32[]{:S(2)}, u32[]{:S(2)}) %collective-permute-start.1) | collective-permute-done | bytes 2097184 | tf_op jit(solution)/shard_map/ppermute | solution.py:38
  64.1 21.5 %collective-permute-done.2 = bf16[512,2048]{1,0:T(8,128)(2,1)} collective-permute-done((bf16[512,2048]{1,0:T(8,128)(2,1)S(1)}, bf16[512,2048]{1,0:T(8,128)(2,1)}, u32[]{:S(2)}, u32[]{:S(2)}) %collective-permute-start.2) | collective-permute-done | bytes 2097184 | tf_op jit(solution)/shard_map/ppermute | solution.py:38
  91.0 20.5 %collective-permute-done.3 = bf16[512,2048]{1,0:T(8,128)(2,1)} collective-permute-done((bf16[512,2048]{1,0:T(8,128)(2,1)}, bf16[512,2048]{1,0:T(8,128)(2,1)}, u32[]{:S(2)}, u32[]{:S(2)}) %collective-permute-start.3) | collective-permute-done | bytes 2097184 | tf_op jit(solution)/shard_map/ppermute | solution.py:38
  126.0 8.0 gather_fusion
  141.6 8.0 gather_fusion.1
  167.3 21.4 %fusion.5 = bf16[16,320,2048]{2,1,0:T(8,128)(2,1)} fusion(bf16[15,64,2048]{2,1,0:T(8,128)(2,1)S(1)} %slice.73, bf16[16,256,2048]{2,1,0:T(8,128)(2,1)} %bitcast.85), kind=kLoop, calls=%fused_computation.17 | loop fusion | flops 62914560 | bytes 41680896 | tf_op jit(solution)/shard_map/concatenate | solution.py:62
  188.9 23.8 %select_convert_fusion = bf16[5120,576]{1,0:T(8,128)(2,1)} fusion(bf16[5120,2048]{1,0:T(8,128)(2,1)} %bitcast.92, f32[576]{0:T(1024)S(1)} %pad_dynamic-slice_fusion.2, f32[5120]{0:T(1024)S(1)} %add.156, pred[576]{0:T(1024)(128)(4,1)S(1)} %add_compare_fusion, pred[5120]{0:T(1024)(128)(4,1)S(1)} %fusion.17, s32[]{:T(128)S(6)} %select_n.81, ...), kind=kOutput, calls=%fused_computation.19 | convolution fusion | flops 12097290240 | bytes 43675460 | tf_op jit(solution)/shard_map/dot_general | solution.py:70
  213.0 85.0 %reduce-scatter.2.cloned.1.call-done = bf16[320,576]{1,0:T(8,128)(2,1)} async-done(((bf16[5120,576]{1,0:T(8,128)(2,1)}), bf16[320,576]{1,0:T(8,128)(2,1)}) %reduce-scatter.2.cloned.1.call-update) | async-done | bytes 368656 | tf_op jit(solution)/shard_map/reduce_scatter | solution.py:75
  301.2 27.6 %while.22 = (s32[]{:T(128)}, f32[32,16,128]{2,1,0:T(8,128)S(1)}, s32[32,16,128]{2,1,0:T(8,128)S(1)}, f32[32,16,256]{2,1,0:T(8,128)S(1)}, s32[]{:T(128)}) while((s32[]{:T(128)}, f32[32,16,128]{2,1,0:T(8,128)S(1)}, s32[32,16,128]{2,1,0:T(8,128)S(1)}, f32[32,16,256]{2,1,0:T(8,128)S(1)}, s32[]{:T(128)}) %tuple.62), condition=%wide.region_4.5_spmd.clone, body=%wide.region_2.4_spmd.clone.sunk | while | flops 1570818 | bytes 98377 | solution.py:95
  329.7 83.3 %all-reduce.6.cloned.1.call-done = f32[512,128]{1,0:T(8,128)} async-done(((f32[512,128]{1,0:T(8,128)}), f32[512,128]{1,0:T(8,128)}) %all-reduce.6.cloned.1.call-update) | async-done | bytes 262160 | tf_op jit(solution)/shard_map/psum | solution.py:104
  415.2 280.2 %while.23 = (s32[]{:T(128)}, f32[32,16,4096]{2,1,0:T(8,128)}, s32[32,16,128]{2,1,0:T(8,128)S(1)}, f32[32,16,128]{2,1,0:T(8,128)S(1)}, s32[]{:T(128)}) while((s32[]{:T(128)}, f32[32,16,4096]{2,1,0:T(8,128)}, s32[32,16,128]{2,1,0:T(8,128)S(1)}, f32[32,16,128]{2,1,0:T(8,128)S(1)}, s32[]{:T(128)}) %tuple.63), condition=%wide.region_9.10_spmd.clone, body=%wide.region_7.9_spmd.clone.sunk | while | flops 25100288 | bytes 836165 | solution.py:114
  424.0 8.0 select_reduce_fusion.6
  432.8 8.0 select_reduce_fusion.6
  441.5 8.0 select_reduce_fusion.6
  450.3 8.0 select_reduce_fusion.6
  459.0 8.0 select_reduce_fusion.6
  467.8 8.0 select_reduce_fusion.6
  476.5 8.0 select_reduce_fusion.6
  485.3 8.0 select_reduce_fusion.6
  494.1 8.0 select_reduce_fusion.6
  502.8 8.0 select_reduce_fusion.6
  511.6 8.0 select_reduce_fusion.6
  520.3 8.0 select_reduce_fusion.6
  529.1 8.0 select_reduce_fusion.6
  537.9 8.0 select_reduce_fusion.6
  546.6 8.0 select_reduce_fusion.6
  555.4 8.0 select_reduce_fusion.6
  564.1 8.0 select_reduce_fusion.6
  572.8 8.0 select_reduce_fusion.6
  581.6 8.0 select_reduce_fusion.6
  590.4 8.0 select_reduce_fusion.6
  599.1 8.0 select_reduce_fusion.6
  607.9 8.0 select_reduce_fusion.6
  616.6 8.0 select_reduce_fusion.6
  625.4 8.0 select_reduce_fusion.6
  634.2 8.0 select_reduce_fusion.6
  651.7 8.0 select_reduce_fusion.6
  660.4 8.0 select_reduce_fusion.6
  669.2 8.0 select_reduce_fusion.6
  695.4 9.2 fusion.49
  704.9 65.8 %psum.29 = f32[32,32]{0,1:T(8,128)S(1)} all-reduce(f32[32,32]{0,1:T(8,128)S(1)} %fusion.36), channel_id=1, replica_groups=mesh['row'=8,'col'=16] {'row','col'}, use_global_device_ids=true, to_apply=%region_10.11 | all-reduce | flops 1024 | bytes 8192 | tf_op jit(solution)/shard_map/psum | solution.py:19
  777.6 63.7 %all_gather.6 = f32[32,4096]{0,1:T(8,128)S(1)} all-gather(f32[32,32]{0,1:T(8,128)S(1)} %fusion.23), channel_id=1, replica_groups=mesh['row'=8,'col'=16] {'row','col'}, dimensions={1}, use_global_device_ids=true | all-gather | bytes 528384 | tf_op jit(solution)/shard_map/all_gather | solution.py:23
  841.3 9.3 fusion.50
  850.8 65.0 %psum.30 = f32[32,32]{0,1:T(8,128)S(1)} all-reduce(f32[32,32]{0,1:T(8,128)S(1)} %fusion.33), channel_id=1, replica_groups=mesh['row'=8,'col'=16] {'row','col'}, use_global_device_ids=true, to_apply=%region_13.16 | all-reduce | flops 1024 | bytes 8192 | tf_op jit(solution)/shard_map/psum | solution.py:19
  922.9 65.1 %all_gather.7 = f32[32,4096]{0,1:T(8,128)S(1)} all-gather(f32[32,32]{0,1:T(8,128)S(1)} %fusion.20), channel_id=1, replica_groups=mesh['row'=8,'col'=16] {'row','col'}, dimensions={1}, use_global_device_ids=true | all-gather | bytes 528384 | tf_op jit(solution)/shard_map/all_gather | solution.py:23
  988.1 9.3 fusion.51
  997.6 65.0 %psum.31 = f32[32,32]{0,1:T(8,128)S(1)} all-reduce(f32[32,32]{0,1:T(8,128)S(1)} %fusion.29), channel_id=1, replica_groups=mesh['row'=8,'col'=16] {'row','col'}, use_global_device_ids=true, to_apply=%region_14.17 | all-reduce | flops 1024 | bytes 8192 | tf_op jit(solution)/shard_map/psum | solution.py:19
  (325 shorter events, 160.1 us)
Async XLA Ops:
  7.2 688.3 %copy-start = (f32[32,4096]{1,0:T(8,128)S(1)}, f32[32,4096]{1,0:T(8,128)}, u32[]{:S(2)}) copy-start(f32[32,4096]{1,0:T(8,128)} %param.12) | copy-start | bytes 1572868
  7.2 290.7 %reduce-scatter.2.cloned.1.call-start = ((), (), s32[]{:S(2)}) async-start(), calls=%async_computation.1 | async-start | bytes 6963200 | tf_op jit(solution)/shard_map/reduce_scatter | solution.py:75
  7.2 26.3 %collective-permute-start = (bf16[512,2048]{1,0:T(8,128)(2,1)}, bf16[512,2048]{1,0:T(8,128)(2,1)S(1)}, u32[]{:S(2)}, u32[]{:S(2)}) collective-permute-start(bf16[512,2048]{1,0:T(8,128)(2,1)} %param.10), channel_id=1, source_target_pairs={{0,16},{16,32},{32,48},{48,64},{64,80},{80,96},{96,112},{112,0},{1... | collective-permute-start | bytes 6291464 | tf_op jit(solution)/shard_map/ppermute | solution.py:38
  33.6 25.4 %collective-permute-start.1 = (bf16[512,2048]{1,0:T(8,128)(2,1)S(1)}, bf16[512,2048]{1,0:T(8,128)(2,1)S(1)}, u32[]{:S(2)}, u32[]{:S(2)}) collective-permute-start(bf16[512,2048]{1,0:T(8,128)(2,1)S(1)} %collective-permute-done), channel_id=1, source_target_pairs={{0,16},{16,32},{32,48},{48,64},{64,80},{80,96},{96,112},{112,0},{1... | collective-permute-start | bytes 6291464 | tf_op jit(solution)/shard_map/ppermute | solution.py:38
  35.9 26.8 %collective-permute-start.4 = (bf16[512,2048]{1,0:T(8,128)(2,1)}, bf16[512,2048]{1,0:T(8,128)(2,1)}, u32[]{:S(2)}, u32[]{:S(2)}) collective-permute-start(bf16[512,2048]{1,0:T(8,128)(2,1)} %param.10), channel_id=1, source_target_pairs={{16,0},{32,16},{48,32},{64,48},{80,64},{96,80},{112,96},{0,112},{1... | collective-permute-start | bytes 6291464 | tf_op jit(solution)/shard_map/ppermute | solution.py:40
  58.9 1.3 copy-start.2
  60.2 25.5 %collective-permute-start.2 = (bf16[512,2048]{1,0:T(8,128)(2,1)S(1)}, bf16[512,2048]{1,0:T(8,128)(2,1)}, u32[]{:S(2)}, u32[]{:S(2)}) collective-permute-start(bf16[512,2048]{1,0:T(8,128)(2,1)S(1)} %collective-permute-done.1), channel_id=1, source_target_pairs={{0,16},{16,32},{32,48},{48,64},{64,80},{80,96},{96,112},{112,0},{1... | collective-permute-start | bytes 6291464 | tf_op jit(solution)/shard_map/ppermute | solution.py:38
  62.7 26.1 %collective-permute-start.5 = (bf16[512,2048]{1,0:T(8,128)(2,1)}, bf16[512,2048]{1,0:T(8,128)(2,1)}, u32[]{:S(2)}, u32[]{:S(2)}) collective-permute-start(bf16[512,2048]{1,0:T(8,128)(2,1)} %collective-permute-done.4), channel_id=1, source_target_pairs={{16,0},{32,16},{48,32},{64,48},{80,64},{96,80},{112,96},{0,112},{1... | collective-permute-start | bytes 6291464 | tf_op jit(solution)/shard_map/ppermute | solution.py:40
  85.7 25.9 %collective-permute-start.3 = (bf16[512,2048]{1,0:T(8,128)(2,1)}, bf16[512,2048]{1,0:T(8,128)(2,1)}, u32[]{:S(2)}, u32[]{:S(2)}) collective-permute-start(bf16[512,2048]{1,0:T(8,128)(2,1)} %collective-permute-done.2), channel_id=1, source_target_pairs={{0,16},{16,32},{32,48},{48,64},{64,80},{80,96},{96,112},{112,0},{1... | collective-permute-start | bytes 6291464 | tf_op jit(solution)/shard_map/ppermute | solution.py:38
  88.3 27.0 %copy-start.3 = (bf16[512,2048]{1,0:T(8,128)(2,1)S(1)}, bf16[512,2048]{1,0:T(8,128)(2,1)}, u32[]{:S(2)}) copy-start(bf16[512,2048]{1,0:T(8,128)(2,1)} %copy-done.2) | copy-start | bytes 6291460
  88.3 27.2 %copy-start.1 = (bf16[512,2048]{1,0:T(8,128)(2,1)S(1)}, bf16[512,2048]{1,0:T(8,128)(2,1)}, u32[]{:S(2)}) copy-start(bf16[512,2048]{1,0:T(8,128)(2,1)} %param.10) | copy-start | bytes 6291460
  88.8 30.6 %collective-permute-start.6 = (bf16[512,2048]{1,0:T(8,128)(2,1)}, bf16[512,2048]{1,0:T(8,128)(2,1)S(1)}, u32[]{:S(2)}, u32[]{:S(2)}) collective-permute-start(bf16[512,2048]{1,0:T(8,128)(2,1)} %collective-permute-done.5), channel_id=1, source_target_pairs={{16,0},{32,16},{48,32},{64,48},{80,64},{96,80},{112,96},{0,112},{1... | collective-permute-start | bytes 6291464 | tf_op jit(solution)/shard_map/ppermute | solution.py:40
  164.7 24.1 %slice-start = ((s8[16777216]{0:T(1024)(128)(4,1)}), s8[4194304]{0:T(1024)(128)(4,1)S(1)}, s32[]{:S(2)}) async-start(s8[16777216]{0:T(1024)(128)(4,1)} %bitcast.86), calls=%async_computation.3 | async-start | bytes 8388608
  167.3 21.6 %slice-start.1 = ((s8[16777216]{0:T(1024)(128)(4,1)}), s8[4194304]{0:T(1024)(128)(4,1)S(1)}, s32[]{:S(2)}) async-start(s8[16777216]{0:T(1024)(128)(4,1)} %bitcast.86), calls=%async_computation.4 | async-start | bytes 8388608
  167.3 21.5 %slice-start.2 = ((s8[16777216]{0:T(1024)(128)(4,1)}), s8[4194304]{0:T(1024)(128)(4,1)S(1)}, s32[]{:S(2)}) async-start(s8[16777216]{0:T(1024)(128)(4,1)} %bitcast.86), calls=%async_computation.5 | async-start | bytes 8388608
  167.3 21.5 %slice-start.3 = ((s8[16777216]{0:T(1024)(128)(4,1)}), s8[4194304]{0:T(1024)(128)(4,1)S(1)}, s32[]{:S(2)}) async-start(s8[16777216]{0:T(1024)(128)(4,1)} %bitcast.86), calls=%async_computation.6 | async-start | bytes 8388608
  188.9 24.0 %copy-start.4 = (s32[512,128]{1,0:T(8,128)S(1)}, s32[512,128]{1,0:T(8,128)}, u32[]{:S(2)}) copy-start(s32[512,128]{1,0:T(8,128)} %param.11) | copy-start | bytes 786436
  212.7 200.3 %all-reduce.6.cloned.1.call-start = ((), (), s32[]{:S(2)}) async-start(), calls=%async_computation.2 | async-start | bytes 524288 | tf_op jit(solution)/shard_map/psum | solution.py:104
Sparse Core Ops, SparseCore 0:
  212.8 85.0 reduce-scatter.1
  329.8 83.1 all-reduce.5
